TPU v7x, 256 devices: a whole 4x4x8 slice. The times are simulated.
256 devices in a mesh: freq: 32 (over x, z_lo, core), mz: 8 (over y, z_hi).
Axes of the slice: x: 4, y: 4, z: 8 (z_hi: 2, z_lo: 4; z = z_hi * 4 + z_lo), core: 2. Of those that a mesh axis runs over, the one named last changes fastest.
Arguments:
- intensity: bfloat16 [8, 6144, 4096], P(None, 'freq', 'mz'), may hold values from -6 to 6
- elution: float32 [6144, 64], P(('freq', 'mz')), may hold values from -6 to 6
- loadings: float32 [8, 64], replicated, may hold values from 0.0005 to 0.01
- shifts: int32 [8, 64], replicated, may hold values from 0 to 255
- bin_weight: float32 [6144], replicated, may hold values from 0.25 to 4
Outputs:
- spectral: float32 [64, 4096], P(None, ('mz', 'freq'))
All inputs are finite; a program needn't handle non-finite values.
Results may differ from a plain program's by a relative error of at most 0.0003.
Values may be sent and summed in bfloat16 or wider, within the bound.
A program may use at most 64 MiB of HBM per device.

v0:
```python
import math
import jax
import jax.numpy as jnp
from jax import lax
from jax.sharding import PartitionSpec as P

PRECISE = lax.Precision.HIGHEST


def turn_angle(product, length):
    return 2.0 * math.pi / length * (product % length).astype(jnp.float32)


def cholesky_solve(gram_matrix, numerator):
    factor = jnp.linalg.cholesky(gram_matrix)
    middle = lax.linalg.triangular_solve(factor, numerator, left_side=True, lower=True)
    return lax.linalg.triangular_solve(factor, middle, left_side=True, lower=True, transpose_a=True)


def on_device(intensity, elution, loadings, shifts, bin_weight):
    freq_count = lax.axis_size("freq")
    mz_count = lax.axis_size("mz")
    freq_rank = lax.axis_index("freq")
    mz_rank = lax.axis_index("mz")
    run_count, bin_count, local_mz = intensity.shape
    length = bin_count * freq_count
    components = loadings.shape[1]
    block_len = bin_count // freq_count
    norm_scale = 1.0 / math.sqrt(length)
    dev_ids = jnp.arange(freq_count, dtype=jnp.int32)
    bin_ids = jnp.arange(bin_count, dtype=jnp.int32)
    dev_angle = turn_angle(dev_ids[:, None] * dev_ids[None, :], freq_count)
    cos_dev = jnp.cos(dev_angle)
    sin_dev = jnp.sin(dev_angle)
    my_times = freq_rank * block_len + jnp.arange(block_len, dtype=jnp.int32)
    twiddle = turn_angle(dev_ids[:, None] * my_times[None, :], length)
    twid_cos = jnp.cos(twiddle)[None, :, :, None]
    twid_sin = jnp.sin(twiddle)[None, :, :, None]
    bin_angle = turn_angle(bin_ids[:, None] * bin_ids[None, :], bin_count)
    cos_bin = jnp.cos(bin_angle)
    sin_bin = jnp.sin(bin_angle)
    full_elution = lax.all_gather(elution, ("freq", "mz"), axis=0, tiled=True)
    stacked = full_elution.reshape(freq_count, bin_count, components)
    weights_grid = bin_weight.reshape(bin_count, freq_count)
    weights_mine = lax.dynamic_slice_in_dim(weights_grid, freq_rank, 1, 1)[:, 0]
    bins_mine = freq_rank + freq_count * bin_ids
    row_angle = turn_angle(freq_rank * dev_ids, freq_count)
    part_re = jnp.einsum("p,pqr->qr", jnp.cos(row_angle), stacked, precision=PRECISE)
    part_im = -jnp.einsum("p,pqr->qr", jnp.sin(row_angle), stacked, precision=PRECISE)
    own_twid = turn_angle(freq_rank * bin_ids, length)[:, None]
    turn_re = part_re * jnp.cos(own_twid) + part_im * jnp.sin(own_twid)
    turn_im = part_im * jnp.cos(own_twid) - part_re * jnp.sin(own_twid)
    own_re = (
        jnp.dot(cos_bin, turn_re, precision=PRECISE) + jnp.dot(sin_bin, turn_im, precision=PRECISE)
    ) * norm_scale
    own_im = (
        jnp.dot(cos_bin, turn_im, precision=PRECISE) - jnp.dot(sin_bin, turn_re, precision=PRECISE)
    ) * norm_scale
    weights_col = weights_mine[None, :, None]

    def own_model(run_amp, run_lag):
        phase = turn_angle(bins_mine[None, :, None] * run_lag[:, None, :], length)
        phase_cos = jnp.cos(phase)
        phase_sin = jnp.sin(phase)
        model_re = run_amp[:, None, :] * (own_re * phase_cos + own_im * phase_sin)
        model_im = run_amp[:, None, :] * (own_im * phase_cos - own_re * phase_sin)
        return (model_re, model_im)

    samples = lax.all_to_all(
        intensity.reshape(run_count, 1, bin_count, local_mz),
        "freq",
        split_axis=2,
        concat_axis=1,
        tiled=True,
    ).astype(jnp.float32)
    raw_re = jnp.einsum("ap,kpim->kaim", cos_dev, samples, precision=PRECISE)
    raw_im = -jnp.einsum("ap,kpim->kaim", sin_dev, samples, precision=PRECISE)
    half_re = raw_re * twid_cos + raw_im * twid_sin
    half_im = raw_im * twid_cos - raw_re * twid_sin
    half_re, half_im = (half_re, half_im)
    piece_re = lax.all_to_all(half_re, "freq", split_axis=1, concat_axis=2, tiled=True)[:, 0]
    piece_im = lax.all_to_all(half_im, "freq", split_axis=1, concat_axis=2, tiled=True)[:, 0]
    out_re = jnp.einsum("bq,kqm->kbm", cos_bin, piece_re, precision=PRECISE) + jnp.einsum(
        "bq,kqm->kbm", sin_bin, piece_im, precision=PRECISE
    )
    out_im = jnp.einsum("bq,kqm->kbm", cos_bin, piece_im, precision=PRECISE) - jnp.einsum(
        "bq,kqm->kbm", sin_bin, piece_re, precision=PRECISE
    )
    model_re, model_im = own_model(loadings, shifts)
    numerator = (
        jnp.einsum("kbr,kbm->rm", weights_col * model_re, out_re, precision=PRECISE)
        + jnp.einsum("kbr,kbm->rm", weights_col * model_im, out_im, precision=PRECISE)
    ) * norm_scale
    run_share = run_count // mz_count
    run_amp = lax.dynamic_slice_in_dim(loadings, mz_rank * run_share, run_share, 0)
    run_lag = lax.dynamic_slice_in_dim(shifts, mz_rank * run_share, run_share, 0)
    model_re, model_im = own_model(run_amp, run_lag)
    gram_matrix = lax.psum(
        jnp.einsum("kbr,kbs->rs", weights_col * model_re, model_re, precision=PRECISE)
        + jnp.einsum("kbr,kbs->rs", weights_col * model_im, model_im, precision=PRECISE),
        ("freq", "mz"),
    )
    owned = lax.psum_scatter(numerator, "freq", scatter_dimension=1, tiled=True)
    return cholesky_solve(gram_matrix, owned)


def solution(mesh):
    in_specs = (P(None, "freq", "mz"), P(("freq", "mz"), None), P(), P(), P())
    out_specs = P(None, ("mz", "freq"))
    return jax.shard_map(
        on_device, mesh=mesh, in_specs=in_specs, out_specs=out_specs, check_vma=False
    )
```

profile of v0, /device:TPU:8, one launch (start us, length us, event | category | flops | bytes accessed | tf_op | source)
XLA Modules:
  0.0 1164.9 jit_solution(4711913364988517103)
XLA Ops:
  6.5 3.4 copy.76
  10.0 8.7 all-to-all-start
  18.9 38.9 %all-to-all-done = bf16[8,1,192,512]{3,0,1,2:T(8,128)(2,1)S(1)} async-done(((bf16[8,1,192,512]{3,0,1,2:T(8,128)(2,1)}), bf16[8,1,192,512]{3,0,1,2:T(8,128)(2,1)S(1)}, u32[]{:S(2)}, u32[]{:S(2)}) %all-to-all-start) | async-done | bytes 1572896 | tf_op jit(solution)/shard_map/all_to_all | solution.py:69
  57.8 3.0 fusion.14
  60.8 5.3 subtract_bitcast_fusion
  66.1 3.5 copy.42
  69.6 4.3 all-to-all-start.1
  73.9 5.4 copy.44
  79.2 67.4 %all-to-all-done.1 = f32[8,32,6,512]{3,0,2,1:T(8,128)S(1)} async-done(((f32[8,32,6,512]{3,0,2,1:T(8,128)}), f32[8,32,6,512]{3,0,2,1:T(8,128)S(1)}, u32[]{:S(2)}, u32[]{:S(2)}) %all-to-all-start.1) | async-done | bytes 3145760 | tf_op jit(solution)/shard_map/all_to_all | solution.py:81
  146.7 4.8 all-to-all-start.2
  151.5 0.7 all-gather.2.cloned.1.call-update
  152.7 692.2 %all-gather.2.cloned.1.call-done = f32[6144,64]{1,0:T(8,128)} async-done(((f32[24,64]{1,0:T(8,128)}), f32[6144,64]{1,0:T(8,128)}) %all-gather.2.cloned.1.call-update) | async-done | bytes 1572880 | tf_op jit(solution)/shard_map/all_gather | solution.py:42
  844.9 2.6 multiply_reduce_fusion
  847.6 1.1 fusion.88
  848.7 1.1 fusion.86
  849.8 1.1 fusion.33
  850.9 1.1 fusion.34
  852.0 0.8 fusion.96
  852.8 0.8 convolution_add_fusion.1
  853.6 105.6 %psum.7 = f32[64,64]{0,1:T(8,128)S(1)} all-reduce(f32[64,64]{0,1:T(8,128)S(1)} %convolution_add_fusion.1), channel_id=1, replica_groups=mesh['freq'=32,'mz'=8] {'freq','mz'}, use_global_device_ids=true, to_apply=%region_0.1 | all-reduce | flops 4096 | bytes 32768 | tf_op jit(solution)/shard_map/psum | solution.py:98
  959.3 5.8 cholesky.16
  965.2 7.3 fusion.12
  972.5 7.4 fusion.10
  980.0 7.5 fusion.8
  987.5 7.7 fusion.6
  995.2 8.6 fusion.18
  1003.8 9.4 fusion.30
  1013.9 0.7 fusion.141
  1014.5 4.9 custom-call.8
  1019.4 136.5 %reduce-scatter.4.cloned.1.call-done = f32[16,64]{1,0:T(8,128)} async-done(((f32[512,64]{1,0:T(8,128)}), f32[16,64]{1,0:T(8,128)}) %reduce-scatter.4.cloned.1.call-update) | async-done | bytes 4112
  1156.0 0.8 fusion.144
  1156.8 0.8 fusion.142
  (27 shorter events, 1.4 us)
Async XLA Ops:
  10.0 47.8 %all-to-all-start = ((bf16[8,1,192,512]{3,0,1,2:T(8,128)(2,1)}), bf16[8,1,192,512]{3,0,1,2:T(8,128)(2,1)S(1)}, u32[]{:S(2)}, u32[]{:S(2)}) async-start(bf16[8,1,192,512]{3,0,1,2:T(8,128)(2,1)} %bitcast.79), calls=%async_computation | async-start | bytes 3145728 | tf_op jit(solution)/shard_map/all_to_all | solution.py:69
  69.6 77.1 %all-to-all-start.1 = ((f32[8,32,6,512]{3,0,2,1:T(8,128)}), f32[8,32,6,512]{3,0,2,1:T(8,128)S(1)}, u32[]{:S(2)}, u32[]{:S(2)}) async-start(f32[8,32,6,512]{3,0,2,1:T(8,128)} %copy.42), calls=%async_computation.1 | async-start | bytes 6291456 | tf_op jit(solution)/shard_map/all_to_all | solution.py:81
  79.2 73.0 %copy-start.2 = (f32[6144]{0:T(1024)S(1)}, f32[6144]{0:T(1024)}, u32[]{:S(2)}) copy-start(f32[6144]{0:T(1024)} %param.9) | copy-start | bytes 73732
  79.2 73.3 %copy-start.4 = (f32[8,64]{1,0:T(8,128)S(1)}, f32[8,64]{1,0:T(8,128)}, u32[]{:S(2)}) copy-start(f32[8,64]{1,0:T(8,128)} %param.7) | copy-start | bytes 6148
  79.2 73.4 %copy-start.3 = (s32[8,64]{1,0:T(8,128)S(1)}, s32[8,64]{1,0:T(8,128)}, u32[]{:S(2)}) copy-start(s32[8,64]{1,0:T(8,128)} %param.8) | copy-start | bytes 6148
  146.7 833.3 %all-to-all-start.2 = ((f32[8,32,6,512]{3,0,2,1:T(8,128)}), f32[8,32,6,512]{3,0,2,1:T(8,128)}, u32[]{:S(2)}, u32[]{:S(2)}) async-start(f32[8,32,6,512]{3,0,2,1:T(8,128)} %copy.44), calls=%async_computation.2 | async-start | bytes 6291456 | tf_op jit(solution)/shard_map/all_to_all | solution.py:82
  151.5 693.4 %all-gather.2.cloned.1.call-start = ((), (), s32[]{:S(2)}) async-start(), calls=%async_computation.4 | async-start | bytes 3158016 | tf_op jit(solution)/shard_map/all_gather | solution.py:42
  152.2 1003.7 %reduce-scatter.4.cloned.1.call-start = ((), (), s32[]{:S(2)}) async-start(), calls=%async_computation.5 | async-start | bytes 270336
  987.5 7.7 copy-start.1
  995.1 8.7 copy-start
Sparse Core Ops, SparseCore 0:
  154.2 690.7 all-gather.1
  1013.4 142.5 reduce-scatter.3
where the time goes:
time: 1170 us; the launch traced here: 1160 us
  waiting for transfers between devices  936 us (80%)
  blocking collectives  106 us (9%)
  matrix products  63.8 us (5%)
  starting transfers between devices  17.9 us (2%)
  other arithmetic  14.9 us (1%)
  between operations  14.1 us (1%)
  local copies, waits for them, and re-layouts  12.7 us (1%)
    all_gather x1, waiting for transfers between devices, on_device(): full_elution = lax.all_gather(elution, ('freq', 'mz'), axis=0, tiled=True)  692 us
    unnamed x3, waiting for transfers between devices  137 us
    psum x1, blocking collectives, on_device(): lax.psum(jnp.einsum('kbr,kbs->rs', weights_col * model_re, model_re, prec...  106 us
    all_to_all x1, waiting for transfers between devices, on_device(): lax.all_to_all(half_re, 'freq', split_axis=1, concat_axis=2, tiled=True)  67.4 us
    all_to_all x1, waiting for transfers between devices, on_device(): lax.all_to_all(intensity.reshape(run_count, 1, bin_count, local_mz), 'fre...  38.9 us
  transfers between devices with their start and end apart: 5, of which 4 were waited for; matrix products, arithmetic and copies ran while one was open for 4% of the time, Pallas kernels for 0%

commit v1 on v0

--- a/solution.py
+++ b/solution.py
@@ -5,6 +5,12 @@
 from jax.sharding import PartitionSpec as P
 
 PRECISE = lax.Precision.HIGHEST
+
+
+def swap_blocks(x, axis, split, join):
+    cells = jnp.split(x, lax.axis_size(axis), axis=split)
+    received = lax.all_to_all(jnp.stack(cells), axis, 0, 0)
+    return jnp.concatenate(received, axis=join)
 
 
 def turn_angle(product, length):
@@ -78,7 +84,7 @@
     half_re = raw_re * twid_cos + raw_im * twid_sin
     half_im = raw_im * twid_cos - raw_re * twid_sin
     half_re, half_im = (half_re, half_im)
-    piece_re = lax.all_to_all(half_re, "freq", split_axis=1, concat_axis=2, tiled=True)[:, 0]
+    piece_re = swap_blocks(half_re, "freq", 1, 2)[:, 0]
     piece_im = lax.all_to_all(half_im, "freq", split_axis=1, concat_axis=2, tiled=True)[:, 0]
     out_re = jnp.einsum("bq,kqm->kbm", cos_bin, piece_re, precision=PRECISE) + jnp.einsum(
         "bq,kqm->kbm", sin_bin, piece_im, precision=PRECISE

time: 1170 us -> 1190 us (1.017)
  local copies, waits for them, and re-layouts: 12.7 us -> 36.6 us
    unnamed x11 -> x44, local copies, waits for them, and re-layouts: 3.45 us -> 27.7 us
where the time goes in v1:
time: 1190 us; the launch traced here: 1180 us
  waiting for transfers between devices  935 us (79%)
  blocking collectives  106 us (9%)
  matrix products  60.1 us (5%)
  local copies, waits for them, and re-layouts  36.6 us (3%)
  starting transfers between devices  17.2 us (1%)
  other arithmetic  14.9 us (1%)
  between operations  14.1 us (1%)
    all_gather x1, waiting for transfers between devices, on_device(): full_elution = lax.all_gather(elution, ('freq', 'mz'), axis=0, tiled=True)  692 us
    unnamed x3, waiting for transfers between devices  137 us
    psum x1, blocking collectives, on_device(): lax.psum(jnp.einsum('kbr,kbs->rs', weights_col * model_re, model_re, prec...  106 us
    all_to_all x1, waiting for transfers between devices, swap_blocks(): received = lax.all_to_all(jnp.stack(cells), axis, 0, 0)  67.4 us
    all_to_all x1, waiting for transfers between devices, on_device(): lax.all_to_all(intensity.reshape(run_count, 1, bin_count, local_mz), 'fre...  38.9 us
    unnamed x44, local copies, waits for them, and re-layouts  27.7 us
  transfers between devices with their start and end apart: 5, of which 4 were waited for; matrix products, arithmetic and copies ran while one was open for 4% of the time, Pallas kernels for 0%

profile of v1, /device:TPU:8, one launch (start us, length us, event | category | flops | bytes accessed | tf_op | source)
XLA Modules:
  0.0 1183.8 jit_solution(16514409751802009263)
XLA Ops:
  6.5 3.4 copy.75
  10.0 8.7 all-to-all-start
  18.9 38.9 %all-to-all-done = bf16[8,1,192,512]{3,0,1,2:T(8,128)(2,1)S(1)} async-done(((bf16[8,1,192,512]{3,0,1,2:T(8,128)(2,1)}), bf16[8,1,192,512]{3,0,1,2:T(8,128)(2,1)S(1)}, u32[]{:S(2)}, u32[]{:S(2)}) %all-to-all-start) | async-done | bytes 1572896 | tf_op jit(solution)/shard_map/all_to_all | solution.py:75
  57.8 3.0 fusion.14
  60.8 5.3 subtract_bitcast_fusion
  87.1 0.7 fusion.97
  89.3 4.3 all-to-all-start.1
  93.6 5.4 copy.43
  99.0 67.4 %all-to-all-done.1 = f32[32,8,1,6,512]{4,2,3,1,0:T(1,128)S(1)} async-done(((f32[32,8,1,6,512]{4,2,3,1,0:T(1,128)}), f32[32,8,1,6,512]{4,2,3,1,0:T(1,128)S(1)}, u32[]{:S(2)}, u32[]{:S(2)}) %all-to-all-start.1) | async-done | bytes 3145760 | tf_op jit(solution)/shard_map/all_to_all | solution.py:12
  166.4 1.6 copy-done
  168.1 4.1 all-to-all-start.2
  173.4 691.6 %all-gather.2.cloned.1.call-done = f32[6144,64]{1,0:T(8,128)} async-done(((f32[24,64]{1,0:T(8,128)}), f32[6144,64]{1,0:T(8,128)}) %all-gather.2.cloned.1.call-update) | async-done | bytes 1572880 | tf_op jit(solution)/shard_map/all_gather | solution.py:48
  865.0 2.6 multiply_reduce_fusion
  867.7 1.1 fusion.88
  868.8 1.1 fusion.86
  869.9 1.1 fusion.33
  871.0 1.1 fusion.34
  872.1 0.8 fusion.128
  872.9 0.8 convolution_add_fusion.1
  873.7 105.7 %psum.7 = f32[64,64]{0,1:T(8,128)S(1)} all-reduce(f32[64,64]{0,1:T(8,128)S(1)} %convolution_add_fusion.1), channel_id=1, replica_groups=mesh['freq'=32,'mz'=8] {'freq','mz'}, use_global_device_ids=true, to_apply=%region_0.1 | all-reduce | flops 4096 | bytes 32768 | tf_op jit(solution)/shard_map/psum | solution.py:104
  979.5 5.8 cholesky.16
  985.3 2.5 copy.41
  987.8 7.3 fusion.12
  995.1 7.5 fusion.10
  1002.6 5.7 fusion.8
  1008.3 5.9 fusion.6
  1014.3 8.4 fusion.18
  1022.7 9.4 fusion.30
  1033.4 4.9 custom-call.8
  1038.3 136.6 %reduce-scatter.4.cloned.1.call-done = f32[16,64]{1,0:T(8,128)} async-done(((f32[512,64]{1,0:T(8,128)}), f32[16,64]{1,0:T(8,128)}) %reduce-scatter.4.cloned.1.call-update) | async-done | bytes 4112
  1174.9 0.8 fusion.176
  1175.8 0.8 fusion.174
  (61 shorter events, 25.3 us)
Async XLA Ops:
  10.0 47.8 %all-to-all-start = ((bf16[8,1,192,512]{3,0,1,2:T(8,128)(2,1)}), bf16[8,1,192,512]{3,0,1,2:T(8,128)(2,1)S(1)}, u32[]{:S(2)}, u32[]{:S(2)}) async-start(bf16[8,1,192,512]{3,0,1,2:T(8,128)(2,1)} %bitcast.208), calls=%async_computation | async-start | bytes 3145728 | tf_op jit(solution)/shard_map/all_to_all | solution.py:75
  89.3 77.1 %all-to-all-start.1 = ((f32[32,8,1,6,512]{4,2,3,1,0:T(1,128)}), f32[32,8,1,6,512]{4,2,3,1,0:T(1,128)S(1)}, u32[]{:S(2)}, u32[]{:S(2)}) async-start(f32[32,8,1,6,512]{4,2,3,1,0:T(1,128)} %fusion.95), calls=%async_computation.1 | async-start | bytes 6291456 | tf_op jit(solution)/shard_map/all_to_all | solution.py:12
  99.0 73.9 %copy-start.3 = (f32[6144]{0:T(1024)S(1)}, f32[6144]{0:T(1024)}, u32[]{:S(2)}) copy-start(f32[6144]{0:T(1024)} %param.9) | copy-start | bytes 73732
  99.0 74.2 %copy-start.5 = (f32[8,64]{1,0:T(8,128)S(1)}, f32[8,64]{1,0:T(8,128)}, u32[]{:S(2)}) copy-start(f32[8,64]{1,0:T(8,128)} %param.7) | copy-start | bytes 6148
  99.0 74.2 %copy-start.4 = (s32[8,64]{1,0:T(8,128)S(1)}, s32[8,64]{1,0:T(8,128)}, u32[]{:S(2)}) copy-start(s32[8,64]{1,0:T(8,128)} %param.8) | copy-start | bytes 6148
  166.4 1.7 copy-start
  168.1 834.5 %all-to-all-start.2 = ((f32[8,32,6,512]{3,0,2,1:T(8,128)}), f32[8,32,6,512]{3,0,2,1:T(8,128)S(1)}, u32[]{:S(2)}, u32[]{:S(2)}) async-start(f32[8,32,6,512]{3,0,2,1:T(8,128)} %copy.43), calls=%async_computation.2 | async-start | bytes 6291456 | tf_op jit(solution)/shard_map/all_to_all | solution.py:88
  172.1 692.9 %all-gather.2.cloned.1.call-start = ((), (), s32[]{:S(2)}) async-start(), calls=%async_computation.4 | async-start | bytes 3158016 | tf_op jit(solution)/shard_map/all_gather | solution.py:48
  172.9 1002.0 %reduce-scatter.4.cloned.1.call-start = ((), (), s32[]{:S(2)}) async-start(), calls=%async_computation.5 | async-start | bytes 270336
  1008.3 5.9 copy-start.2
  1014.3 8.5 copy-start.1
Sparse Core Ops, SparseCore 0:
  174.8 690.1 all-gather.1
  1032.3 142.6 reduce-scatter.3

commit v2 on v0

--- a/solution.py
+++ b/solution.py
@@ -95,11 +95,11 @@
     run_amp = lax.dynamic_slice_in_dim(loadings, mz_rank * run_share, run_share, 0)
     run_lag = lax.dynamic_slice_in_dim(shifts, mz_rank * run_share, run_share, 0)
     model_re, model_im = own_model(run_amp, run_lag)
-    gram_matrix = lax.psum(
-        jnp.einsum("kbr,kbs->rs", weights_col * model_re, model_re, precision=PRECISE)
-        + jnp.einsum("kbr,kbs->rs", weights_col * model_im, model_im, precision=PRECISE),
-        ("freq", "mz"),
-    )
+    gram_matrix = jnp.einsum(
+        "kbr,kbs->rs", weights_col * model_re, model_re, precision=PRECISE
+    ) + jnp.einsum("kbr,kbs->rs", weights_col * model_im, model_im, precision=PRECISE)
+    for name in ("mz", "freq"):
+        gram_matrix = lax.psum(gram_matrix, name)
     owned = lax.psum_scatter(numerator, "freq", scatter_dimension=1, tiled=True)
     return cholesky_solve(gram_matrix, owned)
 

time: 1170 us -> 1280 us (1.094)
  blocking collectives: 106 us -> 212 us
    psum x1 -> x2, blocking collectives: 106 us -> 212 us  [on_device(): gram_matrix = lax.psum(gram_matrix, name)]
  transfers between devices with their start and end apart: 5 -> 5, of which waited for: 4 -> 4; matrix products, arithmetic and copies ran while one was open for 4% -> 3% of each run, Pallas kernels for 0% -> 0%
where the time goes in v2:
time: 1280 us; the launch traced here: 1270 us
  waiting for transfers between devices  932 us (73%)
  blocking collectives  212 us (17%)
  matrix products  63.8 us (5%)
  starting transfers between devices  17.9 us (1%)
  other arithmetic  14.9 us (1%)
  between operations  14.1 us (1%)
    all_gather x1, waiting for transfers between devices, on_device(): full_elution = lax.all_gather(elution, ('freq', 'mz'), axis=0, tiled=True)  692 us
    psum x2, blocking collectives, on_device(): gram_matrix = lax.psum(gram_matrix, name)  212 us
    unnamed x3, waiting for transfers between devices  133 us
    all_to_all x1, waiting for transfers between devices, on_device(): lax.all_to_all(half_re, 'freq', split_axis=1, concat_axis=2, tiled=True)  67.4 us
    all_to_all x1, waiting for transfers between devices, on_device(): lax.all_to_all(intensity.reshape(run_count, 1, bin_count, local_mz), 'fre...  38.9 us
  transfers between devices with their start and end apart: 5, of which 4 were waited for; matrix products, arithmetic and copies ran while one was open for 3% of the time, Pallas kernels for 0%

profile of v2, /device:TPU:8, one launch (start us, length us, event | category | flops | bytes accessed | tf_op | source)
XLA Modules:
  0.0 1267.9 jit_solution(6262598237012247673)
XLA Ops:
  6.5 3.4 copy.76
  10.0 8.7 all-to-all-start
  18.9 38.9 %all-to-all-done = bf16[8,1,192,512]{3,0,1,2:T(8,128)(2,1)S(1)} async-done(((bf16[8,1,192,512]{3,0,1,2:T(8,128)(2,1)}), bf16[8,1,192,512]{3,0,1,2:T(8,128)(2,1)S(1)}, u32[]{:S(2)}, u32[]{:S(2)}) %all-to-all-start) | async-done | bytes 1572896 | tf_op jit(solution)/shard_map/all_to_all | solution.py:69
  57.8 3.0 fusion.14
  60.8 5.3 subtract_bitcast_fusion
  66.1 3.5 copy.42
  69.6 4.3 all-to-all-start.1
  73.9 5.4 copy.44
  79.3 67.4 %all-to-all-done.1 = f32[8,32,6,512]{3,0,2,1:T(8,128)S(1)} async-done(((f32[8,32,6,512]{3,0,2,1:T(8,128)}), f32[8,32,6,512]{3,0,2,1:T(8,128)S(1)}, u32[]{:S(2)}, u32[]{:S(2)}) %all-to-all-start.1) | async-done | bytes 3145760 | tf_op jit(solution)/shard_map/all_to_all | solution.py:81
  146.7 4.8 all-to-all-start.2
  151.6 0.7 all-gather.2.cloned.1.call-update
  152.7 692.2 %all-gather.2.cloned.1.call-done = f32[6144,64]{1,0:T(8,128)} async-done(((f32[24,64]{1,0:T(8,128)}), f32[6144,64]{1,0:T(8,128)}) %all-gather.2.cloned.1.call-update) | async-done | bytes 1572880 | tf_op jit(solution)/shard_map/all_gather | solution.py:42
  845.0 2.6 multiply_reduce_fusion
  847.6 1.1 fusion.88
  848.7 1.1 fusion.86
  849.8 1.1 fusion.33
  850.9 1.1 fusion.34
  852.0 0.8 fusion.96
  852.8 0.8 convolution_add_fusion.1
  853.6 78.8 %psum.14 = f32[64,64]{0,1:T(8,128)S(1)} all-reduce(f32[64,64]{0,1:T(8,128)S(1)} %convolution_add_fusion.1), channel_id=1, replica_groups=mesh['freq'=32,'mz'=8] {'mz'}, use_global_device_ids=true, to_apply=%region_0.1 | all-reduce | flops 4096 | bytes 32768 | tf_op jit(solution)/shard_map/psum | solution.py:102
  932.4 133.6 %psum.15 = f32[64,64]{0,1:T(8,128)S(1)} all-reduce(f32[64,64]{0,1:T(8,128)S(1)} %psum.14), channel_id=1, replica_groups=mesh['freq'=32,'mz'=8] {'freq'}, use_global_device_ids=true, to_apply=%region_1.2 | all-reduce | flops 4096 | bytes 32768 | tf_op jit(solution)/shard_map/psum | solution.py:102
  1066.2 5.8 cholesky.16
  1072.0 7.3 fusion.12
  1079.4 7.4 fusion.10
  1086.8 7.5 fusion.8
  1094.3 7.7 fusion.6
  1102.0 8.6 fusion.18
  1110.6 9.4 fusion.30
  1121.4 4.9 custom-call.8
  1126.2 132.8 %reduce-scatter.4.cloned.1.call-done = f32[16,64]{1,0:T(8,128)} async-done(((f32[512,64]{1,0:T(8,128)}), f32[16,64]{1,0:T(8,128)}) %reduce-scatter.4.cloned.1.call-update) | async-done | bytes 4112
  1259.0 0.8 fusion.144
  1259.8 0.8 fusion.142
  (28 shorter events, 2.0 us)
Async XLA Ops:
  10.0 47.8 %all-to-all-start = ((bf16[8,1,192,512]{3,0,1,2:T(8,128)(2,1)}), bf16[8,1,192,512]{3,0,1,2:T(8,128)(2,1)S(1)}, u32[]{:S(2)}, u32[]{:S(2)}) async-start(bf16[8,1,192,512]{3,0,1,2:T(8,128)(2,1)} %bitcast.79), calls=%async_computation | async-start | bytes 3145728 | tf_op jit(solution)/shard_map/all_to_all | solution.py:69
  69.6 77.1 %all-to-all-start.1 = ((f32[8,32,6,512]{3,0,2,1:T(8,128)}), f32[8,32,6,512]{3,0,2,1:T(8,128)S(1)}, u32[]{:S(2)}, u32[]{:S(2)}) async-start(f32[8,32,6,512]{3,0,2,1:T(8,128)} %copy.42), calls=%async_computation.1 | async-start | bytes 6291456 | tf_op jit(solution)/shard_map/all_to_all | solution.py:81
  79.3 73.0 %copy-start.2 = (f32[6144]{0:T(1024)S(1)}, f32[6144]{0:T(1024)}, u32[]{:S(2)}) copy-start(f32[6144]{0:T(1024)} %param.9) | copy-start | bytes 73732
  79.3 73.3 %copy-start.4 = (f32[8,64]{1,0:T(8,128)S(1)}, f32[8,64]{1,0:T(8,128)}, u32[]{:S(2)}) copy-start(f32[8,64]{1,0:T(8,128)} %param.7) | copy-start | bytes 6148
  79.3 73.3 %copy-start.3 = (s32[8,64]{1,0:T(8,128)S(1)}, s32[8,64]{1,0:T(8,128)}, u32[]{:S(2)}) copy-start(s32[8,64]{1,0:T(8,128)} %param.8) | copy-start | bytes 6148
  146.7 940.1 %all-to-all-start.2 = ((f32[8,32,6,512]{3,0,2,1:T(8,128)}), f32[8,32,6,512]{3,0,2,1:T(8,128)}, u32[]{:S(2)}, u32[]{:S(2)}) async-start(f32[8,32,6,512]{3,0,2,1:T(8,128)} %copy.44), calls=%async_computation.2 | async-start | bytes 6291456 | tf_op jit(solution)/shard_map/all_to_all | solution.py:82
  151.5 693.4 %all-gather.2.cloned.1.call-start = ((), (), s32[]{:S(2)}) async-start(), calls=%async_computation.4 | async-start | bytes 3158016 | tf_op jit(solution)/shard_map/all_gather | solution.py:42
  152.2 1106.8 %reduce-scatter.4.cloned.1.call-start = ((), (), s32[]{:S(2)}) async-start(), calls=%async_computation.5 | async-start | bytes 270336
  1094.3 7.7 copy-start.1
  1102.0 8.7 copy-start
Sparse Core Ops, SparseCore 0:
  154.2 690.7 all-gather.1
  1120.2 138.7 reduce-scatter.3
